TPU v7x, 32 devices: a whole 2x2x4 slice. The times are simulated.
32 devices in a mesh: boxes: 32 (over z, y, x, core).
Axes of the slice: x: 2, y: 2, z: 4, core: 2. Of those that a mesh axis runs over, the one named last changes fastest.
Arguments:
- random_block: bfloat16 [512, 256, 128], P('boxes'), may hold values from -6 to 6
- sample_block: bfloat16 [512, 256, 128], P('boxes'), may hold values from -12 to 12
- near_blocks: bfloat16 [512, 8, 256, 256], P('boxes'), may hold values from -0.375 to 0.375
- near_index: int32 [512, 8], P('boxes'), may hold values from 0 to 511, as said below
- near_count: int32 [512], P('boxes'), may hold values from 2 to 8
Outputs:
- leaf_sketch: bfloat16 [512, 256, 128], P('boxes')
- level_sketch: bfloat16 [32, 9, 128, 128], P('boxes')
Inputs may be any that keep to these rules, and one draw needn't show every extreme that they name: near_index[b, 0] = b; every entry lies within 16 boxes of b; entries at slots from near_count[b] on are ignored.
All inputs are finite; a program needn't handle non-finite values.
Results may differ from a plain program's by a relative error of at most 0.001.
Values may be sent and summed in bfloat16 or wider, within the bound.
A program may use at most 192 MiB of HBM per device.

v0:
```python
import jax
import jax.numpy as jnp
from jax import lax
from jax.sharding import PartitionSpec as P

exact_mode = lax.Precision.HIGHEST


def extended(block, sides, width):
    for axis, dim in sides:
        count = lax.axis_size(axis)
        forward = [(i, i + 1) for i in range(count - 1)]
        backward = [(target, source) for source, target in forward]
        low = lax.ppermute(
            lax.slice_in_dim(block, block.shape[dim] - width, None, axis=dim), axis, forward
        )
        high = lax.ppermute(lax.slice_in_dim(block, 0, width, axis=dim), axis, backward)
        block = jnp.concatenate([low, block, high], axis=dim)
    return block


def inverse_factor(gram):
    size = gram.shape[1]
    if size == 1:
        return 1.0 / jnp.sqrt(gram)
    half = size // 2
    head_inverse = inverse_factor(gram[:, :half, :half])
    lower_block = gram[:, half:, :half]
    cross = jnp.einsum("bij,bkj->bik", lower_block, head_inverse, precision=exact_mode)
    remainder = gram[:, half:, half:] - jnp.einsum(
        "bik,bjk->bij", cross, cross, precision=exact_mode
    )
    tail_inverse = inverse_factor(remainder)
    middle = jnp.einsum("bij,bjk->bik", cross, head_inverse, precision=exact_mode)
    cross_inverse = -jnp.einsum("bij,bjk->bik", tail_inverse, middle, precision=exact_mode)
    zeros_block = jnp.zeros((gram.shape[0], half, size - half), gram.dtype)
    upper_rows = jnp.concatenate([head_inverse, zeros_block], axis=2)
    lower_rows = jnp.concatenate([cross_inverse, tail_inverse], axis=2)
    return jnp.concatenate([upper_rows, lower_rows], axis=1)


def basis_step(sample, random):
    half_width = sample.shape[2] // 2
    compact = sample[:, :, :half_width] + sample[:, :, half_width:]
    gram = jnp.einsum("bik,bil->bkl", compact, compact, precision=exact_mode)
    inverse = inverse_factor(gram)
    rows_q = jnp.einsum("bkl,bil->bki", inverse, compact, precision=exact_mode)
    reduced = jnp.einsum("bki,bis->bks", rows_q, sample, precision=exact_mode)
    projected = jnp.einsum("bki,bis->bks", rows_q, random, precision=exact_mode)
    sketch = jnp.einsum("bki,bks->bis", rows_q, projected, precision=exact_mode)
    return (reduced, projected, sketch)


def merge_pairs(values, nodes):
    return values.reshape(nodes, 2 * values.shape[1], values.shape[2])


def near_masked(wide, local_ids, near_blocks, near_count):
    slots = jnp.arange(near_blocks.shape[1])
    keep_mask = (slots[None, :] < near_count[:, None]).astype(jnp.bfloat16)
    picked = jnp.take(wide, local_ids, axis=0) * keep_mask[:, :, None, None]
    return jnp.einsum("bmij,bmjs->bis", near_blocks, picked, preferred_element_type=jnp.float32)


def per_device(random_block, sample_block, near_blocks, near_index, near_count):
    box_count = random_block.shape[0]
    device = lax.axis_index("boxes")
    wide = extended(random_block, (("boxes", 0),), box_count)
    local_ids = near_index - device * box_count + box_count
    near_sum = near_masked(wide, local_ids, near_blocks, near_count)
    far_sample = sample_block.astype(jnp.float32) - near_sum
    reduced, projected, sketch = basis_step(far_sample, random_block.astype(jnp.float32))
    leaf_sketch = sketch.astype(jnp.bfloat16)
    records = []
    nodes = box_count
    for height in range(box_count.bit_length() - 1):
        nodes = nodes // 2
        reduced, projected, sketch = basis_step(
            merge_pairs(reduced, nodes), merge_pairs(projected, nodes)
        )
        records.append(sketch[0])
    spread = lax.axis_size("boxes").bit_length() - 1
    whole_reduced, whole_projected = (
        lax.all_gather(reduced, "boxes", axis=0, tiled=True),
        lax.all_gather(projected, "boxes", axis=0, tiled=True),
    )
    nodes = lax.axis_size("boxes")
    for height in range(spread):
        nodes = nodes // 2
        whole_reduced, whole_projected, sketch = basis_step(
            merge_pairs(whole_reduced, nodes), merge_pairs(whole_projected, nodes)
        )
        records.append(
            lax.dynamic_index_in_dim(sketch, device // 2 ** (height + 1), 0, keepdims=False)
        )
    level_sketch = jnp.stack(records, axis=0)[None].astype(jnp.bfloat16)
    return (leaf_sketch, level_sketch)


def solution(mesh):
    return jax.shard_map(
        per_device,
        mesh=mesh,
        in_specs=(
            P("boxes", None, None),
            P("boxes", None, None),
            P("boxes", None, None, None),
            P("boxes", None),
            P("boxes"),
        ),
        out_specs=(P("boxes", None, None), P("boxes", None, None, None)),
        check_vma=False,
    )
```

profile of v0, /device:TPU:0, one launch (start us, length us, event | category | flops | bytes accessed | tf_op | source)
XLA Modules:
  0.0 790.2 jit_solution(14415660442587407392)
XLA Ops:
  7.2 2.5 collective-permute-start
  9.7 1.3 collective-permute-start.1
  12.0 2.3 copy.7049
  14.2 0.7 fusion.2507
  15.0 1.0 copy-done.4
  16.6 2.0 pad_maximum_fusion
  18.6 6.6 gather_fusion
  25.2 12.4 %copy.7052 = bf16[16,8,256,128]{2,3,1,0:T(8,128)(2,1)} copy(bf16[16,8,256,128]{3,2,1,0:T(8,128)(2,1)} %bitcast.4573) | data formatting | bytes 16777216 | tf_op jit(solution)/shard_map/jit(_take)/gather | solution.py:61
  37.6 11.4 %bitcast_subtract_fusion = f32[16,256,128]{1,2,0:T(8,128)S(1)} fusion(bf16[16,256,128]{1,2,0:T(8,128)(2,1)S(1)} %copy-done.3, bf16[16,8,256,256]{3,2,1,0:T(8,128)(2,1)} %param.7, bf16[16,8,256,128]{2,3,1,0:T(8,128)(2,1)} %copy.7052, pred[16,8]{1,0:T(8,128)(4,1)S(1)} %copy.7050, bf16[16,8]{1,0:T(8,128)(2,1)S(1)} %fusion.2507), kind=kOutput, calls=%fused_computation.8 | convolution fusion | flops 2156920832 | bytes 28311936 | tf_op jit(solution)/shard_map/bmij,bmjs->bis/dot_general | solution.py:62
  49.0 1.1 fusion.186
  81.7 1.1 fusion.5334
  114.5 2.5 fusion.138
  117.0 3.9 fusion.5336
  262.1 0.7 fusion.5303
  265.8 0.7 fusion.5271
  269.2 0.7 fusion.5302
  273.3 0.7 fusion.5255
  276.7 0.7 fusion.5301
  280.5 0.7 fusion.5270
  283.8 0.7 fusion.5300
  288.4 0.7 fusion.5247
  291.7 0.7 fusion.5299
  295.5 0.7 fusion.5269
  298.8 0.7 fusion.5298
  303.0 0.7 fusion.5254
  306.3 0.7 fusion.5297
  310.1 0.7 fusion.5268
  313.5 0.7 fusion.5296
  321.6 0.7 fusion.5295
  325.4 0.7 fusion.5267
  328.8 0.7 fusion.5294
  333.1 0.7 fusion.5253
  336.4 0.7 fusion.5293
  340.2 0.7 fusion.5266
  343.6 0.7 fusion.5292
  348.1 0.7 fusion.5246
  351.5 0.7 fusion.5291
  355.2 0.7 fusion.5265
  358.6 0.7 fusion.5290
  362.7 0.7 fusion.5252
  366.1 0.7 fusion.5289
  369.8 0.7 fusion.5264
  373.2 0.7 fusion.5288
  378.7 0.8 fusion.5443
  380.1 1.0 fusion.5370
  381.8 0.8 fusion.5442
  383.6 4.7 convolution_convert_fusion
  388.7 65.1 %all-gather.5.cloned.1.call-done = f32[2048,128]{1,0:T(8,128)} async-done(((f32[64,128]{1,0:T(8,128)}), f32[2048,128]{1,0:T(8,128)}) %all-gather.5.cloned.1.call-update) | async-done | bytes 1048592 | tf_op jit(solution)/shard_map/all_gather | solution.py:84
  453.7 2.0 fusion.5233
  456.4 0.9 fusion.5444
  521.1 0.8 fusion.136
  521.9 1.1 fusion.5478
  664.2 0.7 fusion.5287
  667.8 0.7 fusion.5263
  681.7 0.7 fusion.5262
  684.9 0.7 fusion.5284
  692.4 0.7 fusion.5283
  709.9 0.7 fusion.5260
  713.0 0.7 fusion.5280
  720.7 0.7 fusion.5279
  727.5 0.7 fusion.5278
  774.4 2.3 fusion.5476
  776.7 1.8 fusion.5477
  779.1 1.2 fusion.5512
  (3551 shorter events, 480.2 us)
Async XLA Ops:
  7.2 446.5 %all-gather.5.cloned.1.call-start = ((), (), s32[]{:S(2)}) async-start(), calls=%async_computation | async-start | bytes 1081344 | tf_op jit(solution)/shard_map/all_gather | solution.py:84
  7.2 7.8 collective-permute-start
  9.7 6.9 collective-permute-start.1
  15.0 1.0 copy-start.4
  25.2 12.4 %copy-start.3 = (bf16[16,256,128]{1,2,0:T(8,128)(2,1)S(1)}, bf16[16,256,128]{1,2,0:T(8,128)(2,1)}, u32[]{:S(2)}) copy-start(bf16[16,256,128]{1,2,0:T(8,128)(2,1)} %copy.7049) | copy-start | bytes 3145732
  49.0 65.5 %copy-start.1 = (f32[16,256,128]{1,2,0:T(8,128)}, f32[16,256,128]{1,2,0:T(8,128)S(1)}, u32[]{:S(2)}) copy-start(f32[16,256,128]{1,2,0:T(8,128)S(1)} %bitcast_subtract_fusion) | copy-start | bytes 6291460
  98.7 15.3 %copy-start.6 = (f32[16,32,32]{2,1,0:T(8,128)S(1)}, f32[16,32,32]{2,1,0:T(8,128)}, u32[]{:S(2)}) copy-start(f32[16,32,32]{2,1,0:T(8,128)} %fusion.5334) | copy-start | bytes 196612
  111.6 2.3 copy-start.8
  111.6 2.3 copy-start.9
  111.7 2.3 copy-start.7
  112.3 1.7 copy-start.10
  112.4 1.6 copy-start.11
  234.6 140.7 %copy-start.2 = (bf16[16,256,128]{2,1,0:T(8,128)(2,1)S(1)}, bf16[16,256,128]{2,1,0:T(8,128)(2,1)}, u32[]{:S(2)}) copy-start(bf16[16,256,128]{2,1,0:T(8,128)(2,1)} %param.5) | copy-start | bytes 3145732
  379.5 394.9 %all-gather.7.cloned.1.call-start = ((), (), s32[]{:S(2)}) async-start(), calls=%async_computation.1 | async-start | bytes 1081344 | tf_op jit(solution)/shard_map/all_gather | solution.py:85
  382.6 5.8 copy-start.5
  518.3 3.6 copy-start
  782.5 0.7 copy-start.12
Sparse Core Ops, SparseCore 0:
  379.6 74.0 all-gather.4
  457.1 53.1 all-gather.6
where the time goes:
time: 796 us; the launch traced here: 790 us
  matrix products  305 us (38%)
  local copies, waits for them, and re-layouts  170 us (21%)
  between operations  150 us (19%)
  other arithmetic  94.5 us (12%)
  waiting for transfers between devices  65.7 us (8%)
    dot_general x310, matrix products, inverse_factor(): jnp.einsum('bij,bjk->bik', tail_inverse, middle, precision=exact_mode)  85.8 us
    all_gather x1, waiting for transfers between devices, per_device(): lax.all_gather(reduced, 'boxes', axis=0, tiled=True)  65.1 us
    dot_general x310, matrix products, inverse_factor(): jnp.einsum('bij,bkj->bik', lower_block, head_inverse, precision=exact_mode)  64.6 us
    dot_general x310, matrix products, inverse_factor(): jnp.einsum('bij,bjk->bik', cross, head_inverse, precision=exact_mode)  56.5 us
    sqrt x256, other arithmetic, inverse_factor(): return 1.0 / jnp.sqrt(gram)  56.4 us
    dot_general x310, matrix products, inverse_factor(): jnp.einsum('bik,bjk->bij', cross, cross, precision=exact_mode)  50.2 us
    slice x64, local copies, waits for them, and re-layouts, inverse_factor(): head_inverse = inverse_factor(gram[:, :half, :half])  45.9 us
    sqrt x256, local copies, waits for them, and re-layouts, inverse_factor(): return 1.0 / jnp.sqrt(gram)  41.8 us
  transfers between devices with their start and end apart: 4, of which 2 were waited for; matrix products, arithmetic and copies ran while one was open for 34% of the time, Pallas kernels for 0%

commit v1 on v0

v1 whole, which is shorter than its diff:
```python
import functools

import jax
import jax.numpy as jnp
from jax import lax
from jax.experimental import pallas as pl
from jax.experimental.pallas import tpu as pltpu
from jax.sharding import PartitionSpec as P

exact_mode = lax.Precision.HIGHEST


def exact_dot(a, b):
    return jnp.dot(a, b, precision=exact_mode, preferred_element_type=jnp.float32)


def gram_kernel(ids, counts, blocks, sample, low, own, high, grams, compact, wide, sems):
    box = pl.program_id(0)
    count = own.shape[0]
    slots, samples = blocks.shape[1], sample.shape[2]
    half = samples // 2

    @pl.when(box == 0)
    def _():
        copies = [
            pltpu.make_async_copy(part, wide.at[pl.ds(place * count, count)], sems.at[place])
            for place, part in enumerate((low, own, high))
        ]
        for copy in copies:
            copy.start()
        for copy in copies:
            copy.wait()

    total = jnp.zeros(sample.shape[1:], jnp.float32)
    for slot in range(slots):
        keep = (slot < counts[box]).astype(jnp.float32).astype(jnp.bfloat16)
        picked = wide[ids[box * slots + slot]] * keep
        total += jnp.dot(blocks[0, slot], picked, preferred_element_type=jnp.float32)
    far = sample[0].astype(jnp.float32) - total
    doubled = far + pltpu.roll(far, half, 1)
    compact[0] = doubled
    random = wide[count + box].astype(jnp.float32)
    flipped = doubled.T[:half]
    grams[0] = exact_dot(flipped, jnp.concatenate([doubled, random], axis=1))


def gram_call(ids, counts, blocks, sample, low, own, high):
    count, rows, samples = sample.shape
    slots = blocks.shape[1]
    half = samples // 2
    anywhere = pl.BlockSpec(memory_space=pl.ANY)
    return pl.pallas_call(
        gram_kernel,
        grid_spec=pltpu.PrefetchScalarGridSpec(
            num_scalar_prefetch=2,
            grid=(count,),
            in_specs=[
                pl.BlockSpec((1, slots, rows, rows), lambda b, *_: (b, 0, 0, 0)),
                pl.BlockSpec((1, rows, samples), lambda b, *_: (b, 0, 0)),
                anywhere,
                anywhere,
                anywhere,
            ],
            out_specs=[
                pl.BlockSpec((1, half, 2 * samples), lambda b, *_: (b, 0, 0)),
                pl.BlockSpec((1, rows, samples), lambda b, *_: (b, 0, 0)),
            ],
            scratch_shapes=[
                pltpu.VMEM((3 * count, rows, samples), jnp.bfloat16),
                pltpu.SemaphoreType.DMA((3,)),
            ],
        ),
        out_shape=[
            jax.ShapeDtypeStruct((count, half, 2 * samples), jnp.float32),
            jax.ShapeDtypeStruct((count, rows, samples), jnp.float32),
        ],
        name="gram",
    )(ids, counts, blocks, sample, low, own, high)


def eliminate(total, half, work, uppers, with_upper):
    samples = 2 * half
    lanes = lax.broadcasted_iota(jnp.int32, (1, samples), 1)

    def step(k, carry):
        at_k = lanes == k
        for node in range(total):
            matrix = work[node]
            row = work[node, pl.ds(k, 1), :]
            column = jnp.sum(jnp.where(at_k, matrix, 0.0), axis=1, keepdims=True)
            pivot = jnp.sum(jnp.where(at_k, row, 0.0), axis=1, keepdims=True)
            scaled = row / pivot
            work[node] = matrix - column * scaled
            work[node, pl.ds(k, 1), :] = scaled
            if node in with_upper:
                kept = (lanes >= k) & (lanes < half)
                uppers[with_upper[node], pl.ds(k, 1), :] = jnp.where(
                    kept, row * lax.rsqrt(pivot), 0.0
                )
        return carry

    lax.fori_loop(0, half, step, 0)


def start_matrix(gram, half):
    samples = 2 * half
    rows = lax.broadcasted_iota(jnp.int32, (half, samples), 0)
    lanes = lax.broadcasted_iota(jnp.int32, (half, samples), 1)
    return jnp.where(lanes < half, gram, (lanes - half == rows).astype(jnp.float32))


def solved(work, node, moment):
    blank = jnp.zeros_like(moment)
    answer = exact_dot(work[node], jnp.concatenate([blank, moment], axis=0))
    return jnp.concatenate([answer, blank], axis=0)


def local_kernel(grams, compact, leaf_out, level_out, work, moments, uppers):
    count = grams.shape[0]
    half, samples = grams.shape[1], grams.shape[2] // 2
    depth = count.bit_length() - 1
    total = work.shape[0]
    for node in range(count):
        work[node] = start_matrix(grams[node, :, :samples], half)
    spans = []
    for height in range(1, depth + 1):
        spans += [(0, 2**height)] if height == depth else [(0, 2**height), (2**height, 2 ** (height + 1))]
    for place, (first, last) in enumerate(spans):
        summed = grams[first]
        for leaf in range(first + 1, last):
            summed = summed + grams[leaf]
        work[count + place] = start_matrix(summed[:, :samples], half)
        moments[place] = summed[:, samples:]
    with_upper = {0: 0, 1: 1}
    for height in range(1, depth):
        for side in range(2):
            with_upper[count + 2 * (height - 1) + side] = 2 * height + side
    eliminate(total, half, work, uppers, with_upper)
    for leaf in range(count):
        answer = solved(work, leaf, grams[leaf, :, samples:])
        leaf_out[leaf] = exact_dot(compact[leaf], answer).astype(leaf_out.dtype)
    for height in range(1, depth + 1):
        place = 2 * (height - 1)
        answer = solved(work, count + place, moments[place])
        stacked = jnp.concatenate([uppers[place], uppers[place + 1]], axis=0)
        level_out[height - 1] = exact_dot(stacked, answer).astype(level_out.dtype)


def local_call(grams, compact):
    count, half, double = grams.shape
    samples = double // 2
    depth = count.bit_length() - 1
    extra = 2 * depth - 1
    return pl.pallas_call(
        local_kernel,
        out_shape=[
            jax.ShapeDtypeStruct(compact.shape, jnp.bfloat16),
            jax.ShapeDtypeStruct((depth, samples, samples), jnp.bfloat16),
        ],
        scratch_shapes=[
            pltpu.VMEM((count + extra, half, samples), jnp.float32),
            pltpu.VMEM((extra, half, samples), jnp.float32),
            pltpu.VMEM((2 * depth, half, samples), jnp.float32),
        ],
        cost_estimate=pl.CostEstimate(
            flops=500_000_000, bytes_accessed=4_000_000, transcendentals=0
        ),
        name="local",
    )(grams, compact)


def upper_kernel(nodes, level_out, work, uppers):
    total = nodes.shape[0]
    half, samples = nodes.shape[1], nodes.shape[2] // 2
    for node in range(total):
        work[node] = start_matrix(nodes[node, :, :samples], half)
    eliminate(total, half, work, uppers, {node: node for node in range(total - 1)})


def upper_solve(nodes, picks, level_out, work, uppers):
    upper_kernel(nodes, level_out, work, uppers)
    total = nodes.shape[0]
    samples = nodes.shape[2] // 2
    spread = (total - 1) // 2
    for height in range(spread):
        if height == spread - 1:
            answer = solved(work, total - 1, nodes[total - 1, :, samples:])
        else:
            mine = picks[height + 1]
            place = 2 * (height + 1) + mine
            answer = solved(work, place, nodes[place, :, samples:])
        stacked = jnp.concatenate([uppers[2 * height], uppers[2 * height + 1]], axis=0)
        level_out[height] = exact_dot(stacked, answer).astype(level_out.dtype)


def upper_call(nodes, picks):
    total, half, double = nodes.shape
    samples = double // 2
    spread = (total - 1) // 2
    return pl.pallas_call(
        upper_solve,
        in_specs=[
            pl.BlockSpec(memory_space=pltpu.VMEM),
            pl.BlockSpec(memory_space=pltpu.SMEM),
        ],
        out_shape=jax.ShapeDtypeStruct((spread, samples, samples), jnp.bfloat16),
        scratch_shapes=[
            pltpu.VMEM((total, half, samples), jnp.float32),
            pltpu.VMEM((total - 1, half, samples), jnp.float32),
        ],
        name="upper",
    )(nodes, picks)


def per_device(random_block, sample_block, near_blocks, near_index, near_count):
    count = random_block.shape[0]
    device = lax.axis_index("boxes")
    size = lax.axis_size("boxes")
    forward = [(i, i + 1) for i in range(size - 1)]
    backward = [(target, source) for source, target in forward]
    low = lax.ppermute(random_block, "boxes", forward)
    high = lax.ppermute(random_block, "boxes", backward)
    ids = jnp.clip(near_index - device * count + count, 0, 3 * count - 1).reshape(-1)
    grams, compact = gram_call(
        ids, near_count, near_blocks, sample_block, low, random_block, high
    )
    summed = jnp.sum(grams, axis=0)
    nodes = []
    spread = size.bit_length() - 1
    bits = (device >> jnp.arange(spread)) & 1
    for step in range(spread):
        other = lax.ppermute(summed, "boxes", [(i, i ^ (1 << step)) for i in range(size)])
        odd = bits[step] == 1
        nodes += [jnp.where(odd, other, summed), jnp.where(odd, summed, other)]
        summed = summed + other
    nodes.append(summed)
    leaf_sketch, level_low = local_call(grams, compact)
    level_high = upper_call(jnp.stack(nodes), bits.astype(jnp.int32))
    return (leaf_sketch, jnp.concatenate([level_low, level_high], axis=0)[None])


def solution(mesh):
    return jax.shard_map(
        per_device,
        mesh=mesh,
        in_specs=(
            P("boxes", None, None),
            P("boxes", None, None),
            P("boxes", None, None, None),
            P("boxes", None),
            P("boxes"),
        ),
        out_specs=(P("boxes", None, None), P("boxes", None, None, None)),
        check_vma=False,
    )
```

time: 796 us -> 285 us (0.36)
  matrix products: 305 us -> 0 us
  Pallas kernels: 0 us -> 226 us
  local copies, waits for them, and re-layouts: 170 us -> 3.2 us
  between operations: 150 us -> 3.98 us
  other arithmetic: 94.5 us -> 3.87 us
  waiting for transfers between devices: 65.7 us -> 16.1 us
  starting transfers between devices: 3.84 us -> 30.6 us
    dot_general x1290 -> x0, matrix products: 305 us -> none  [the longest x310 85.8 us: inverse_factor(): jnp.einsum('bij,bjk->bik', tail_inverse, middle, precision=exact_mode)]
    pallas_call x0 -> x3, Pallas kernels: none -> 226 us  [the longest x1 138 us: local_call(): pl.pallas_call(local_kernel, out_shape=[jax.ShapeDtypeStruct(compact.shap...]
    all_gather x2 -> x0, waiting for transfers between devices: 65.1 us -> none  [the longest x1 65.1 us: per_device(): lax.all_gather(reduced, 'boxes', axis=0, tiled=True)]
    sqrt x256 -> x0, other arithmetic: 56.4 us -> none  [inverse_factor(): return 1.0 / jnp.sqrt(gram)]
    slice x71 -> x1, local copies, waits for them, and re-layouts: 48.8 us -> 0.66 us  [per_device(): odd = bits[step] == 1]
    sqrt x256 -> x0, local copies, waits for them, and re-layouts: 41.8 us -> none  [inverse_factor(): return 1.0 / jnp.sqrt(gram)]
    concatenate x311 -> x0, other arithmetic: 31.8 us -> none  [the longest x310 29.8 us: inverse_factor(): return jnp.concatenate([upper_rows, lower_rows], axis=1)]
    neg x312 -> x0, local copies, waits for them, and re-layouts: 28.4 us -> none  [inverse_factor(): -jnp.einsum('bij,bjk->bik', tail_inverse, middle, precision=exact_mode)]
  transfers between devices with their start and end apart: 4 -> 7, of which waited for: 2 -> 5; matrix products, arithmetic and copies ran while one was open for 34% -> 1% of each run, Pallas kernels for 0% -> 49%
where the time goes in v1:
time: 285 us; the launch traced here: 284 us
  Pallas kernels  226 us (79%)
  starting transfers between devices  30.6 us (11%)
  waiting for transfers between devices  16.1 us (6%)
  between operations  3.98 us (1%)
  other arithmetic  3.87 us (1%)
  local copies, waits for them, and re-layouts  3.2 us (1%)
    pallas_call x1, Pallas kernels, local_call(): pl.pallas_call(local_kernel, out_shape=[jax.ShapeDtypeStruct(compact.shap...  138 us
    pallas_call x1, Pallas kernels, upper_call(): pl.pallas_call(upper_solve, in_specs=[pl.BlockSpec(memory_space=pltpu.VME...  66.3 us
    ppermute x5, starting transfers between devices, per_device(): lax.ppermute(summed, 'boxes', [(i, i ^ 1 << step) for i in range(size)])  26.9 us
    pallas_call x1, Pallas kernels, gram_call(): pl.pallas_call(gram_kernel, grid_spec=pltpu.PrefetchScalarGridSpec(num_sc...  21.7 us
    ppermute x5, waiting for transfers between devices, per_device(): lax.ppermute(summed, 'boxes', [(i, i ^ 1 << step) for i in range(size)])  12 us
  transfers between devices with their start and end apart: 7, of which 5 were waited for; matrix products, arithmetic and copies ran while one was open for 1% of the time, Pallas kernels for 49%

profile of v1, /device:TPU:0, one launch (start us, length us, event | category | flops | bytes accessed | tf_op | source)
XLA Modules:
  0.0 283.9 jit_solution(511461501697359378)
XLA Ops:
  0.6 2.5 collective-permute-start
  3.1 1.3 collective-permute-start.1
  4.4 0.7 add_clamp_fusion
  5.1 0.1 copy.8
  5.2 0.6 reshape.17.ids
  5.8 0.0 copy-start.3
  5.8 0.0 collective-permute-done.low
  5.8 0.0 copy-start
  5.8 4.1 %collective-permute-done.1.high = bf16[16,256,128]{2,1,0:T(8,128)(2,1)S(1)} collective-permute-done((bf16[16,256,128]{2,1,0:T(8,128)(2,1)}, bf16[16,256,128]{2,1,0:T(8,128)(2,1)S(1)}, u32[]{:S(2)}, u32[]{:S(2)}) %collective-permute-start.1) | collective-permute-done | bytes 1048608 | tf_op jit(solution)/shard_map/ppermute | solution.py:222
  9.9 0.0 copy-done
  9.9 0.0 copy-start.1
  9.9 1.0 copy-done.1
  10.9 21.7 %gram.1 = (f32[16,64,256]{2,1,0:T(8,128)}, f32[16,256,128]{2,1,0:T(8,128)}) custom-call(s32[128]{0:T(128)} %reshape.17.ids, s32[16]{0:T(128)} %counts.1, bf16[16,8,256,256]{3,2,1,0:T(8,128)(2,1)} %blocks.1, bf16[16,256,128]{2,1,0:T(8,128)(2,1)} %sample.1, bf16[16,256,128]{2,1,0:T(8,128)(2,1)} %copy-done, bf16[16,256,128]{2,1,0:T(8,128)(2,1)} %own.1, ...), custom_call_target="tpu_custom_call" | custom-call | tf_op jit(solution)/shard_map/gram/pallas_call | solution.py:52
  32.6 1.3 reduce_sum.9
  33.9 20.6 %collective-permute-start.2 = (f32[64,256]{1,0:T(8,128)S(1)}, f32[64,256]{1,0:T(8,128)S(1)}, u32[]{:S(2)}, u32[]{:S(2)}) collective-permute-start(f32[64,256]{1,0:T(8,128)S(1)} %reduce_sum.9), channel_id=1, source_target_pairs={{0,1},{1,0},{2,3},{3,2},{4,5},{5,4},{6,7},{7,6},{8,9},{9,8},{10,11... | collective-permute-start | bytes 196616 | tf_op jit(solution)/shard_map/ppermute | solution.py:232
  54.5 0.7 fusion
  58.4 138.1 %local.1 = (bf16[16,256,128]{2,1,0:T(8,128)(2,1)}, bf16[4,128,128]{2,1,0:T(8,128)(2,1)}) custom-call(f32[16,64,256]{2,1,0:T(8,128)} %get-tuple-element.6.grams, f32[16,256,128]{2,1,0:T(8,128)} %get-tuple-element.7.compact), custom_call_target="tpu_custom_call" | custom-call | flops 500000000 | bytes 4000000 | tf_op jit(solution)/shard_map/local/pallas_call | solution.py:154
  196.5 0.0 collective-permute-done.2
  196.5 1.8 collective-permute-start.3
  198.3 2.7 collective-permute-done.3
  201.0 0.1 collective-permute-start.4
  201.2 4.2 %collective-permute-done.4 = f32[64,256]{1,0:T(8,128)S(1)} collective-permute-done((f32[64,256]{1,0:T(8,128)S(1)}, f32[64,256]{1,0:T(8,128)S(1)}, u32[]{:S(2)}, u32[]{:S(2)}) %collective-permute-start.4) | collective-permute-done | bytes 65568 | tf_op jit(solution)/shard_map/ppermute | solution.py:232
  205.4 1.6 collective-permute-start.5
  207.1 2.7 collective-permute-done.5
  209.7 2.8 collective-permute-start.6
  212.6 2.4 collective-permute-done.6
  215.0 0.0 copy-done.3
  215.0 0.0 copy-start.2
  215.0 0.9 copy-done.2
  215.9 66.3 %upper.1 = bf16[5,128,128]{2,1,0:T(8,128)(2,1)} custom-call(f32[11,64,256]{2,1,0:T(8,128)} %copy-done.2, s32[5]{0:T(128)} %copy-done.3), custom_call_target="tpu_custom_call" | custom-call | tf_op jit(solution)/shard_map/upper/pallas_call | solution.py:200
  282.2 1.7 maximum_bitcast_fusion
  (16 shorter events, 0.2 us)
Async XLA Ops:
  0.6 5.2 %collective-permute-start = (bf16[16,256,128]{2,1,0:T(8,128)(2,1)}, bf16[16,256,128]{2,1,0:T(8,128)(2,1)S(1)}, u32[]{:S(2)}, u32[]{:S(2)}) collective-permute-start(bf16[16,256,128]{2,1,0:T(8,128)(2,1)} %own.1), channel_id=1, source_target_pairs={{0,1},{1,2},{2,3},{3,4},{4,5},{5,6},{6,7},{7,8},{8,9},{9,10},{10,1... | collective-permute-start | bytes 3145736 | tf_op jit(solution)/shard_map/ppermute | solution.py:221
  3.1 6.8 %collective-permute-start.1 = (bf16[16,256,128]{2,1,0:T(8,128)(2,1)}, bf16[16,256,128]{2,1,0:T(8,128)(2,1)S(1)}, u32[]{:S(2)}, u32[]{:S(2)}) collective-permute-start(bf16[16,256,128]{2,1,0:T(8,128)(2,1)} %own.1), channel_id=1, source_target_pairs={{1,0},{2,1},{3,2},{4,3},{5,4},{6,5},{7,6},{8,7},{9,8},{10,9},{11,1... | collective-permute-start | bytes 3145736 | tf_op jit(solution)/shard_map/ppermute | solution.py:222
  5.8 209.2 %copy-start.3 = (s32[5]{0:T(128)}, s32[5]{0:T(128)S(1)}, u32[]{:S(2)}) copy-start(s32[5]{0:T(128)S(1)} %shift-right-arithmetic_and_fusion.picks) | copy-start | bytes 64
  5.8 4.1 %copy-start = (bf16[16,256,128]{2,1,0:T(8,128)(2,1)}, bf16[16,256,128]{2,1,0:T(8,128)(2,1)S(1)}, u32[]{:S(2)}) copy-start(bf16[16,256,128]{2,1,0:T(8,128)(2,1)S(1)} %collective-permute-done.low) | copy-start | bytes 3145732
  9.9 1.0 copy-start.1
  33.9 162.6 %collective-permute-start.2 = (f32[64,256]{1,0:T(8,128)S(1)}, f32[64,256]{1,0:T(8,128)S(1)}, u32[]{:S(2)}, u32[]{:S(2)}) collective-permute-start(f32[64,256]{1,0:T(8,128)S(1)} %reduce_sum.9), channel_id=1, source_target_pairs={{0,1},{1,0},{2,3},{3,2},{4,5},{5,4},{6,7},{7,6},{8,9},{9,8},{10,11... | collective-permute-start | bytes 196616 | tf_op jit(solution)/shard_map/ppermute | solution.py:232
  196.5 4.5 %collective-permute-start.3 = (f32[64,256]{1,0:T(8,128)S(1)}, f32[64,256]{1,0:T(8,128)S(1)}, u32[]{:S(2)}, u32[]{:S(2)}) collective-permute-start(f32[64,256]{1,0:T(8,128)S(1)} %add.23), channel_id=1, source_target_pairs={{0,2},{1,3},{2,0},{3,1},{4,6},{5,7},{6,4},{7,5},{8,10},{9,11},{10,... | collective-permute-start | bytes 196616 | tf_op jit(solution)/shard_map/ppermute | solution.py:232
  201.0 4.3 %collective-permute-start.4 = (f32[64,256]{1,0:T(8,128)S(1)}, f32[64,256]{1,0:T(8,128)S(1)}, u32[]{:S(2)}, u32[]{:S(2)}) collective-permute-start(f32[64,256]{1,0:T(8,128)S(1)} %add.24), channel_id=1, source_target_pairs={{0,4},{1,5},{2,6},{3,7},{4,0},{5,1},{6,2},{7,3},{8,12},{9,13},{10,... | collective-permute-start | bytes 196616 | tf_op jit(solution)/shard_map/ppermute | solution.py:232
  205.4 4.3 %collective-permute-start.5 = (f32[64,256]{1,0:T(8,128)S(1)}, f32[64,256]{1,0:T(8,128)S(1)}, u32[]{:S(2)}, u32[]{:S(2)}) collective-permute-start(f32[64,256]{1,0:T(8,128)S(1)} %add.25), channel_id=1, source_target_pairs={{0,8},{1,9},{2,10},{3,11},{4,12},{5,13},{6,14},{7,15},{8,0},{9,1},... | collective-permute-start | bytes 196616 | tf_op jit(solution)/shard_map/ppermute | solution.py:232
  209.7 5.2 %collective-permute-start.6 = (f32[64,256]{1,0:T(8,128)S(1)}, f32[64,256]{1,0:T(8,128)S(1)}, u32[]{:S(2)}, u32[]{:S(2)}) collective-permute-start(f32[64,256]{1,0:T(8,128)S(1)} %add.26), channel_id=1, source_target_pairs={{0,16},{1,17},{2,18},{3,19},{4,20},{5,21},{6,22},{7,23},{8,24},{9,... | collective-permute-start | bytes 196616 | tf_op jit(solution)/shard_map/ppermute | solution.py:232
  215.0 0.9 copy-start.2

commit v2 on v1

--- a/solution.py
+++ b/solution.py
@@ -31,39 +31,42 @@
         for copy in copies:
             copy.wait()
 
-    total = jnp.zeros(sample.shape[1:], jnp.float32)
-    for slot in range(slots):
-        keep = (slot < counts[box]).astype(jnp.float32).astype(jnp.bfloat16)
-        picked = wide[ids[box * slots + slot]] * keep
-        total += jnp.dot(blocks[0, slot], picked, preferred_element_type=jnp.float32)
-    far = sample[0].astype(jnp.float32) - total
-    doubled = far + pltpu.roll(far, half, 1)
-    compact[0] = doubled
-    random = wide[count + box].astype(jnp.float32)
-    flipped = doubled.T[:half]
-    grams[0] = exact_dot(flipped, jnp.concatenate([doubled, random], axis=1))
+    for part in range(blocks.shape[0]):
+        here = box * blocks.shape[0] + part
+        total = jnp.zeros(sample.shape[1:], jnp.float32)
+        for slot in range(slots):
+            keep = (slot < counts[here]).astype(jnp.float32).astype(jnp.bfloat16)
+            picked = wide[ids[here * slots + slot]] * keep
+            total += jnp.dot(blocks[part, slot], picked, preferred_element_type=jnp.float32)
+        far = sample[part].astype(jnp.float32) - total
+        doubled = far + pltpu.roll(far, half, 1)
+        compact[part] = doubled
+        random = wide[count + here].astype(jnp.float32)
+        flipped = doubled.T[:half]
+        grams[part] = exact_dot(flipped, jnp.concatenate([doubled, random], axis=1))
 
 
 def gram_call(ids, counts, blocks, sample, low, own, high):
     count, rows, samples = sample.shape
     slots = blocks.shape[1]
     half = samples // 2
+    together = 2 if count % 2 == 0 else 1
     anywhere = pl.BlockSpec(memory_space=pl.ANY)
     return pl.pallas_call(
         gram_kernel,
         grid_spec=pltpu.PrefetchScalarGridSpec(
             num_scalar_prefetch=2,
-            grid=(count,),
+            grid=(count // together,),
             in_specs=[
-                pl.BlockSpec((1, slots, rows, rows), lambda b, *_: (b, 0, 0, 0)),
-                pl.BlockSpec((1, rows, samples), lambda b, *_: (b, 0, 0)),
+                pl.BlockSpec((together, slots, rows, rows), lambda b, *_: (b, 0, 0, 0)),
+                pl.BlockSpec((together, rows, samples), lambda b, *_: (b, 0, 0)),
                 anywhere,
                 anywhere,
                 anywhere,
             ],
             out_specs=[
-                pl.BlockSpec((1, half, 2 * samples), lambda b, *_: (b, 0, 0)),
-                pl.BlockSpec((1, rows, samples), lambda b, *_: (b, 0, 0)),
+                pl.BlockSpec((together, half, 2 * samples), lambda b, *_: (b, 0, 0)),
+                pl.BlockSpec((together, rows, samples), lambda b, *_: (b, 0, 0)),
             ],
             scratch_shapes=[
                 pltpu.VMEM((3 * count, rows, samples), jnp.bfloat16),
@@ -82,21 +85,31 @@
     samples = 2 * half
     lanes = lax.broadcasted_iota(jnp.int32, (1, samples), 1)
 
+    rows = lax.broadcasted_iota(jnp.int32, (half, samples), 0)
+    group = 4
+
     def step(k, carry):
         at_k = lanes == k
-        for node in range(total):
-            matrix = work[node]
-            row = work[node, pl.ds(k, 1), :]
-            column = jnp.sum(jnp.where(at_k, matrix, 0.0), axis=1, keepdims=True)
-            pivot = jnp.sum(jnp.where(at_k, row, 0.0), axis=1, keepdims=True)
-            scaled = row / pivot
-            work[node] = matrix - column * scaled
-            work[node, pl.ds(k, 1), :] = scaled
-            if node in with_upper:
-                kept = (lanes >= k) & (lanes < half)
-                uppers[with_upper[node], pl.ds(k, 1), :] = jnp.where(
-                    kept, row * lax.rsqrt(pivot), 0.0
-                )
+        kept = (lanes >= k) & (lanes < half)
+        row_k = rows == k
+        pivots = [work[node, pl.ds(k, 1), :] for node in range(total)]
+        picked = [
+            jnp.sum(jnp.where(at_k, row, 0.0), axis=1, keepdims=True) for row in pivots
+        ]
+        scaled = [row / pivot for row, pivot in zip(pivots, picked)]
+        for node, place in with_upper.items():
+            uppers[place, pl.ds(k, 1), :] = jnp.where(
+                kept, pivots[node] * lax.rsqrt(picked[node]), 0.0
+            )
+        for first in range(0, total, group):
+            members = range(first, min(first + group, total))
+            matrices = [work[node] for node in members]
+            columns = [
+                jnp.sum(jnp.where(at_k, matrix, 0.0), axis=1, keepdims=True)
+                for matrix in matrices
+            ]
+            for node, matrix, column in zip(members, matrices, columns):
+                work[node] = jnp.where(row_k, scaled[node], matrix - column * scaled[node])
         return carry
 
     lax.fori_loop(0, half, step, 0)

time: 285 us -> 118 us (0.41)
  Pallas kernels: 226 us -> 59.4 us
    pallas_call x1, Pallas kernels: 138 us -> 26.2 us  [local_call(): pl.pallas_call(local_kernel, out_shape=[jax.ShapeDtypeStruct(compact.shap...]
    pallas_call x1, Pallas kernels: 66.3 us -> 15.4 us  [upper_call(): pl.pallas_call(upper_solve, in_specs=[pl.BlockSpec(memory_space=pltpu.VME...]
    pallas_call x1, Pallas kernels: 21.7 us -> 17.7 us  [gram_call(): pl.pallas_call(gram_kernel, grid_spec=pltpu.PrefetchScalarGridSpec(num_sc...]
  transfers between devices with their start and end apart: 7 -> 7, of which waited for: 5 -> 5; matrix products, arithmetic and copies ran while one was open for 1% -> 2% of each run, Pallas kernels for 49% -> 22%
where the time goes in v2:
time: 118 us; the launch traced here: 117 us
  Pallas kernels  59.4 us (50%)
  starting transfers between devices  30.6 us (26%)
  waiting for transfers between devices  16.1 us (14%)
  between operations  3.98 us (3%)
  other arithmetic  3.87 us (3%)
  local copies, waits for them, and re-layouts  3.2 us (3%)
    ppermute x5, starting transfers between devices, per_device(): lax.ppermute(summed, 'boxes', [(i, i ^ 1 << step) for i in range(size)])  26.9 us
    pallas_call x1, Pallas kernels, local_call(): pl.pallas_call(local_kernel, out_shape=[jax.ShapeDtypeStruct(compact.shap...  26.2 us
    pallas_call x1, Pallas kernels, gram_call(): pl.pallas_call(gram_kernel, grid_spec=pltpu.PrefetchScalarGridSpec(num_sc...  17.7 us
    pallas_call x1, Pallas kernels, upper_call(): pl.pallas_call(upper_solve, in_specs=[pl.BlockSpec(memory_space=pltpu.VME...  15.4 us
    ppermute x5, waiting for transfers between devices, per_device(): lax.ppermute(summed, 'boxes', [(i, i ^ 1 << step) for i in range(size)])  12 us
    ppermute x1, waiting for transfers between devices, per_device(): high = lax.ppermute(random_block, 'boxes', backward)  4.1 us
    ppermute x1, starting transfers between devices, per_device(): low = lax.ppermute(random_block, 'boxes', forward)  2.47 us
  transfers between devices with their start and end apart: 7, of which 5 were waited for; matrix products, arithmetic and copies ran while one was open for 2% of the time, Pallas kernels for 22%

profile of v2, /device:TPU:0, one launch (start us, length us, event | category | flops | bytes accessed | tf_op | source)
XLA Modules:
  0.0 117.2 jit_solution(11958187163171865978)
XLA Ops:
  0.6 2.5 %collective-permute-start = (bf16[16,256,128]{2,1,0:T(8,128)(2,1)}, bf16[16,256,128]{2,1,0:T(8,128)(2,1)S(1)}, u32[]{:S(2)}, u32[]{:S(2)}) collective-permute-start(bf16[16,256,128]{2,1,0:T(8,128)(2,1)} %own.1), channel_id=1, source_target_pairs={{0,1},{1,2},{2,3},{3,4},{4,5},{5,6},{6,7},{7,8},{8,9},{9,10},{10,1... | collective-permute-start | bytes 3145736 | tf_op jit(solution)/shard_map/ppermute | solution.py:234
  3.1 1.3 %collective-permute-start.1 = (bf16[16,256,128]{2,1,0:T(8,128)(2,1)}, bf16[16,256,128]{2,1,0:T(8,128)(2,1)S(1)}, u32[]{:S(2)}, u32[]{:S(2)}) collective-permute-start(bf16[16,256,128]{2,1,0:T(8,128)(2,1)} %own.1), channel_id=1, source_target_pairs={{1,0},{2,1},{3,2},{4,3},{5,4},{6,5},{7,6},{8,7},{9,8},{10,9},{11,1... | collective-permute-start | bytes 3145736 | tf_op jit(solution)/shard_map/ppermute | solution.py:235
  4.4 0.7 add_clamp_fusion
  5.1 0.1 copy.8
  5.2 0.6 reshape.17.ids
  5.8 0.0 copy-start.3
  5.8 0.0 collective-permute-done.low
  5.8 0.0 copy-start
  5.8 4.1 %collective-permute-done.1.high = bf16[16,256,128]{2,1,0:T(8,128)(2,1)S(1)} collective-permute-done((bf16[16,256,128]{2,1,0:T(8,128)(2,1)}, bf16[16,256,128]{2,1,0:T(8,128)(2,1)S(1)}, u32[]{:S(2)}, u32[]{:S(2)}) %collective-permute-start.1) | collective-permute-done | bytes 1048608 | tf_op jit(solution)/shard_map/ppermute | solution.py:235
  9.9 0.0 copy-done
  9.9 0.0 copy-start.1
  9.9 1.0 copy-done.1
  10.9 17.7 %gram.1 = (f32[16,64,256]{2,1,0:T(8,128)}, f32[16,256,128]{2,1,0:T(8,128)}) custom-call(s32[128]{0:T(128)} %reshape.17.ids, s32[16]{0:T(128)} %counts.1, bf16[16,8,256,256]{3,2,1,0:T(8,128)(2,1)} %blocks.1, bf16[16,256,128]{2,1,0:T(8,128)(2,1)} %sample.1, bf16[16,256,128]{2,1,0:T(8,128)(2,1)} %copy-done, bf16[16,256,128]{2,1,0:T(8,128)(2,1)} %own.1, ...), custom_call_target="tpu_custom_call" | custom-call | tf_op jit(solution)/shard_map/gram/pallas_call | solution.py:55
  28.6 1.3 %reduce_sum.9 = f32[64,256]{1,0:T(8,128)S(1)} reduce(f32[16,64,256]{2,1,0:T(8,128)} %get-tuple-element.6.grams, f32[]{:T(128)} %constant.21.clone.1), dimensions={0}, to_apply=%region_0.1 | reduce | flops 245760 | bytes 1114116 | tf_op jit(solution)/shard_map/reduce_sum | solution.py:240
  29.9 20.6 %collective-permute-start.2 = (f32[64,256]{1,0:T(8,128)S(1)}, f32[64,256]{1,0:T(8,128)S(1)}, u32[]{:S(2)}, u32[]{:S(2)}) collective-permute-start(f32[64,256]{1,0:T(8,128)S(1)} %reduce_sum.9), channel_id=1, source_target_pairs={{0,1},{1,0},{2,3},{3,2},{4,5},{5,4},{6,7},{7,6},{8,9},{9,8},{10,11... | collective-permute-start | bytes 196616 | tf_op jit(solution)/shard_map/ppermute | solution.py:245
  50.5 0.7 fusion
  54.4 26.2 %local.1 = (bf16[16,256,128]{2,1,0:T(8,128)(2,1)}, bf16[4,128,128]{2,1,0:T(8,128)(2,1)}) custom-call(f32[16,64,256]{2,1,0:T(8,128)} %get-tuple-element.6.grams, f32[16,256,128]{2,1,0:T(8,128)} %get-tuple-element.7.compact), custom_call_target="tpu_custom_call" | custom-call | flops 500000000 | bytes 4000000 | tf_op jit(solution)/shard_map/local/pallas_call | solution.py:167
  80.6 0.0 collective-permute-done.2
  80.6 1.8 %collective-permute-start.3 = (f32[64,256]{1,0:T(8,128)S(1)}, f32[64,256]{1,0:T(8,128)S(1)}, u32[]{:S(2)}, u32[]{:S(2)}) collective-permute-start(f32[64,256]{1,0:T(8,128)S(1)} %add.23), channel_id=1, source_target_pairs={{0,2},{1,3},{2,0},{3,1},{4,6},{5,7},{6,4},{7,5},{8,10},{9,11},{10,... | collective-permute-start | bytes 196616 | tf_op jit(solution)/shard_map/ppermute | solution.py:245
  82.4 2.7 %collective-permute-done.3 = f32[64,256]{1,0:T(8,128)S(1)} collective-permute-done((f32[64,256]{1,0:T(8,128)S(1)}, f32[64,256]{1,0:T(8,128)S(1)}, u32[]{:S(2)}, u32[]{:S(2)}) %collective-permute-start.3) | collective-permute-done | bytes 65568 | tf_op jit(solution)/shard_map/ppermute | solution.py:245
  85.2 0.1 collective-permute-start.4
  85.3 4.2 %collective-permute-done.4 = f32[64,256]{1,0:T(8,128)S(1)} collective-permute-done((f32[64,256]{1,0:T(8,128)S(1)}, f32[64,256]{1,0:T(8,128)S(1)}, u32[]{:S(2)}, u32[]{:S(2)}) %collective-permute-start.4) | collective-permute-done | bytes 65568 | tf_op jit(solution)/shard_map/ppermute | solution.py:245
  89.5 1.6 %collective-permute-start.5 = (f32[64,256]{1,0:T(8,128)S(1)}, f32[64,256]{1,0:T(8,128)S(1)}, u32[]{:S(2)}, u32[]{:S(2)}) collective-permute-start(f32[64,256]{1,0:T(8,128)S(1)} %add.25), channel_id=1, source_target_pairs={{0,8},{1,9},{2,10},{3,11},{4,12},{5,13},{6,14},{7,15},{8,0},{9,1},... | collective-permute-start | bytes 196616 | tf_op jit(solution)/shard_map/ppermute | solution.py:245
  91.2 2.7 %collective-permute-done.5 = f32[64,256]{1,0:T(8,128)S(1)} collective-permute-done((f32[64,256]{1,0:T(8,128)S(1)}, f32[64,256]{1,0:T(8,128)S(1)}, u32[]{:S(2)}, u32[]{:S(2)}) %collective-permute-start.5) | collective-permute-done | bytes 65568 | tf_op jit(solution)/shard_map/ppermute | solution.py:245
  93.9 2.8 %collective-permute-start.6 = (f32[64,256]{1,0:T(8,128)S(1)}, f32[64,256]{1,0:T(8,128)S(1)}, u32[]{:S(2)}, u32[]{:S(2)}) collective-permute-start(f32[64,256]{1,0:T(8,128)S(1)} %add.26), channel_id=1, source_target_pairs={{0,16},{1,17},{2,18},{3,19},{4,20},{5,21},{6,22},{7,23},{8,24},{9,... | collective-permute-start | bytes 196616 | tf_op jit(solution)/shard_map/ppermute | solution.py:245
  96.7 2.4 %collective-permute-done.6 = f32[64,256]{1,0:T(8,128)S(1)} collective-permute-done((f32[64,256]{1,0:T(8,128)S(1)}, f32[64,256]{1,0:T(8,128)S(1)}, u32[]{:S(2)}, u32[]{:S(2)}) %collective-permute-start.6) | collective-permute-done | bytes 65568 | tf_op jit(solution)/shard_map/ppermute | solution.py:245
  99.1 0.0 copy-done.3
  99.1 0.0 copy-start.2
  99.2 0.9 copy-done.2
  100.0 15.4 %upper.1 = bf16[5,128,128]{2,1,0:T(8,128)(2,1)} custom-call(f32[11,64,256]{2,1,0:T(8,128)} %copy-done.2, s32[5]{0:T(128)} %copy-done.3), custom_call_target="tpu_custom_call" | custom-call | tf_op jit(solution)/shard_map/upper/pallas_call | solution.py:213
  115.5 1.7 %maximum_bitcast_fusion = bf16[1,9,128,128]{3,2,1,0:T(8,128)(2,1)} fusion(bf16[5,128,128]{2,1,0:T(8,128)(2,1)} %upper.1, bf16[4,128,128]{2,1,0:T(8,128)(2,1)} %get-tuple-element.9), kind=kLoop, calls=%fused_computation | loop fusion | flops 147456 | bytes 589824 | tf_op jit(solution)/shard_map/broadcast_in_dim | solution.py:252
  (16 shorter events, 0.2 us)
Async XLA Ops:
  0.6 5.2 %collective-permute-start = (bf16[16,256,128]{2,1,0:T(8,128)(2,1)}, bf16[16,256,128]{2,1,0:T(8,128)(2,1)S(1)}, u32[]{:S(2)}, u32[]{:S(2)}) collective-permute-start(bf16[16,256,128]{2,1,0:T(8,128)(2,1)} %own.1), channel_id=1, source_target_pairs={{0,1},{1,2},{2,3},{3,4},{4,5},{5,6},{6,7},{7,8},{8,9},{9,10},{10,1... | collective-permute-start | bytes 3145736 | tf_op jit(solution)/shard_map/ppermute | solution.py:234
  3.1 6.8 %collective-permute-start.1 = (bf16[16,256,128]{2,1,0:T(8,128)(2,1)}, bf16[16,256,128]{2,1,0:T(8,128)(2,1)S(1)}, u32[]{:S(2)}, u32[]{:S(2)}) collective-permute-start(bf16[16,256,128]{2,1,0:T(8,128)(2,1)} %own.1), channel_id=1, source_target_pairs={{1,0},{2,1},{3,2},{4,3},{5,4},{6,5},{7,6},{8,7},{9,8},{10,9},{11,1... | collective-permute-start | bytes 3145736 | tf_op jit(solution)/shard_map/ppermute | solution.py:235
  5.8 93.4 %copy-start.3 = (s32[5]{0:T(128)}, s32[5]{0:T(128)S(1)}, u32[]{:S(2)}) copy-start(s32[5]{0:T(128)S(1)} %shift-right-arithmetic_and_fusion.picks) | copy-start | bytes 64
  5.8 4.1 %copy-start = (bf16[16,256,128]{2,1,0:T(8,128)(2,1)}, bf16[16,256,128]{2,1,0:T(8,128)(2,1)S(1)}, u32[]{:S(2)}) copy-start(bf16[16,256,128]{2,1,0:T(8,128)(2,1)S(1)} %collective-permute-done.low) | copy-start | bytes 3145732
  9.9 1.0 copy-start.1
  29.9 50.7 %collective-permute-start.2 = (f32[64,256]{1,0:T(8,128)S(1)}, f32[64,256]{1,0:T(8,128)S(1)}, u32[]{:S(2)}, u32[]{:S(2)}) collective-permute-start(f32[64,256]{1,0:T(8,128)S(1)} %reduce_sum.9), channel_id=1, source_target_pairs={{0,1},{1,0},{2,3},{3,2},{4,5},{5,4},{6,7},{7,6},{8,9},{9,8},{10,11... | collective-permute-start | bytes 196616 | tf_op jit(solution)/shard_map/ppermute | solution.py:245
  80.6 4.5 %collective-permute-start.3 = (f32[64,256]{1,0:T(8,128)S(1)}, f32[64,256]{1,0:T(8,128)S(1)}, u32[]{:S(2)}, u32[]{:S(2)}) collective-permute-start(f32[64,256]{1,0:T(8,128)S(1)} %add.23), channel_id=1, source_target_pairs={{0,2},{1,3},{2,0},{3,1},{4,6},{5,7},{6,4},{7,5},{8,10},{9,11},{10,... | collective-permute-start | bytes 196616 | tf_op jit(solution)/shard_map/ppermute | solution.py:245
  85.2 4.3 %collective-permute-start.4 = (f32[64,256]{1,0:T(8,128)S(1)}, f32[64,256]{1,0:T(8,128)S(1)}, u32[]{:S(2)}, u32[]{:S(2)}) collective-permute-start(f32[64,256]{1,0:T(8,128)S(1)} %add.24), channel_id=1, source_target_pairs={{0,4},{1,5},{2,6},{3,7},{4,0},{5,1},{6,2},{7,3},{8,12},{9,13},{10,... | collective-permute-start | bytes 196616 | tf_op jit(solution)/shard_map/ppermute | solution.py:245
  89.5 4.3 %collective-permute-start.5 = (f32[64,256]{1,0:T(8,128)S(1)}, f32[64,256]{1,0:T(8,128)S(1)}, u32[]{:S(2)}, u32[]{:S(2)}) collective-permute-start(f32[64,256]{1,0:T(8,128)S(1)} %add.25), channel_id=1, source_target_pairs={{0,8},{1,9},{2,10},{3,11},{4,12},{5,13},{6,14},{7,15},{8,0},{9,1},... | collective-permute-start | bytes 196616 | tf_op jit(solution)/shard_map/ppermute | solution.py:245
  93.9 5.2 %collective-permute-start.6 = (f32[64,256]{1,0:T(8,128)S(1)}, f32[64,256]{1,0:T(8,128)S(1)}, u32[]{:S(2)}, u32[]{:S(2)}) collective-permute-start(f32[64,256]{1,0:T(8,128)S(1)} %add.26), channel_id=1, source_target_pairs={{0,16},{1,17},{2,18},{3,19},{4,20},{5,21},{6,22},{7,23},{8,24},{9,... | collective-permute-start | bytes 196616 | tf_op jit(solution)/shard_map/ppermute | solution.py:245
  99.1 0.9 copy-start.2

commit v3 on v2

--- a/solution.py
+++ b/solution.py
@@ -81,7 +81,7 @@
     )(ids, counts, blocks, sample, low, own, high)
 
 
-def eliminate(total, half, work, uppers, with_upper):
+def eliminate(nodes, low_k, high_k, half, work, uppers, with_upper):
     samples = 2 * half
     lanes = lax.broadcasted_iota(jnp.int32, (1, samples), 1)
 
@@ -92,17 +92,18 @@
         at_k = lanes == k
         kept = (lanes >= k) & (lanes < half)
         row_k = rows == k
-        pivots = [work[node, pl.ds(k, 1), :] for node in range(total)]
-        picked = [
-            jnp.sum(jnp.where(at_k, row, 0.0), axis=1, keepdims=True) for row in pivots
-        ]
-        scaled = [row / pivot for row, pivot in zip(pivots, picked)]
+        pivots = {node: work[node, pl.ds(k, 1), :] for node in nodes}
+        picked = {
+            node: jnp.sum(jnp.where(at_k, pivots[node], 0.0), axis=1, keepdims=True)
+            for node in nodes
+        }
+        scaled = {node: pivots[node] / picked[node] for node in nodes}
         for node, place in with_upper.items():
             uppers[place, pl.ds(k, 1), :] = jnp.where(
                 kept, pivots[node] * lax.rsqrt(picked[node]), 0.0
             )
-        for first in range(0, total, group):
-            members = range(first, min(first + group, total))
+        for first in range(0, len(nodes), group):
+            members = nodes[first : first + group]
             matrices = [work[node] for node in members]
             columns = [
                 jnp.sum(jnp.where(at_k, matrix, 0.0), axis=1, keepdims=True)
@@ -112,7 +113,7 @@
                 work[node] = jnp.where(row_k, scaled[node], matrix - column * scaled[node])
         return carry
 
-    lax.fori_loop(0, half, step, 0)
+    lax.fori_loop(low_k, high_k, step, 0)
 
 
 def start_matrix(gram, half):
@@ -128,27 +129,70 @@
     return jnp.concatenate([answer, blank], axis=0)
 
 
-def local_kernel(grams, compact, leaf_out, level_out, work, moments, uppers):
+def tree_kernel(
+    spread, grams, compact, leaf_out, level_out, work, moments, uppers, sums, arrived, sent, landed
+):
     count = grams.shape[0]
     half, samples = grams.shape[1], grams.shape[2] // 2
     depth = count.bit_length() - 1
-    total = work.shape[0]
+    me = lax.axis_index("boxes")
+    bits = [lax.rem(lax.div(me, 1 << step), 2) for step in range(spread)]
+    partners = [me + (1 - 2 * bit) * (1 << step) for step, bit in enumerate(bits)]
+    barrier = pltpu.get_barrier_semaphore()
+    for partner in partners:
+        pl.semaphore_signal(
+            barrier, inc=1, device_id=(partner,), device_id_type=pl.DeviceIdType.MESH
+        )
+    summed = grams[0]
+    for leaf in range(1, count):
+        summed = summed + grams[leaf]
+    sums[0] = summed
+
+    def exchange(step):
+        return pltpu.make_async_remote_copy(
+            src_ref=sums.at[step],
+            dst_ref=arrived.at[step],
+            send_sem=sent.at[step],
+            recv_sem=landed.at[step],
+            device_id=(partners[step],),
+            device_id_type=pl.DeviceIdType.MESH,
+        )
+
+    pl.semaphore_wait(barrier, spread)
+    copies = [exchange(step) for step in range(spread)]
+    copies[0].start()
     for node in range(count):
         work[node] = start_matrix(grams[node, :, :samples], half)
-    spans = []
+    place = 0
     for height in range(1, depth + 1):
-        spans += [(0, 2**height)] if height == depth else [(0, 2**height), (2**height, 2 ** (height + 1))]
-    for place, (first, last) in enumerate(spans):
-        summed = grams[first]
-        for leaf in range(first + 1, last):
-            summed = summed + grams[leaf]
-        work[count + place] = start_matrix(summed[:, :samples], half)
-        moments[place] = summed[:, samples:]
+        for side in range(1 if height == depth else 2):
+            first = side * 2**height
+            part = grams[first]
+            for leaf in range(first + 1, first + 2**height):
+                part = part + grams[leaf]
+            work[count + place] = start_matrix(part[:, :samples], half)
+            moments[place] = part[:, samples:]
+            place += 1
+    below = count + place
     with_upper = {0: 0, 1: 1}
-    for height in range(1, depth):
-        for side in range(2):
-            with_upper[count + 2 * (height - 1) + side] = 2 * height + side
-    eliminate(total, half, work, uppers, with_upper)
+    for node in range(place):
+        with_upper[count + node] = 2 + node
+    own = 1 + place
+    nodes = list(range(below))
+    for step in range(spread):
+        eliminate(
+            nodes, half * step // spread, half * (step + 1) // spread, half, work, uppers, with_upper
+        )
+        copies[step].wait()
+        sums[step + 1] = sums[step] + arrived[step]
+        if step + 1 < spread:
+            copies[step + 1].start()
+    for step in range(spread):
+        work[below + 2 * step] = start_matrix(arrived[step, :, :samples], half)
+        work[below + 2 * step + 1] = start_matrix(sums[step + 1, :, :samples], half)
+    nodes = list(range(below, below + 2 * spread))
+    later = {node: own + 1 + node - below for node in nodes[:-1]}
+    eliminate(nodes, 0, half, half, work, uppers, later)
     for leaf in range(count):
         answer = solved(work, leaf, grams[leaf, :, samples:])
         leaf_out[leaf] = exact_dot(compact[leaf], answer).astype(leaf_out.dtype)
@@ -156,73 +200,42 @@
         place = 2 * (height - 1)
         answer = solved(work, count + place, moments[place])
         stacked = jnp.concatenate([uppers[place], uppers[place + 1]], axis=0)
-        level_out[height - 1] = exact_dot(stacked, answer).astype(level_out.dtype)
-
-
-def local_call(grams, compact):
+        level_out[0, height - 1] = exact_dot(stacked, answer).astype(level_out.dtype)
+    for step in range(spread):
+        mine, other = uppers[own + 2 * step], uppers[own + 2 * step + 1]
+        odd = bits[step] == 1
+        stacked = jnp.concatenate(
+            [jnp.where(odd, other, mine), jnp.where(odd, mine, other)], axis=0
+        )
+        answer = solved(work, below + 2 * step + 1, sums[step + 1, :, samples:])
+        level_out[0, depth + step] = exact_dot(stacked, answer).astype(level_out.dtype)
+
+
+def tree_call(grams, compact, spread):
     count, half, double = grams.shape
     samples = double // 2
     depth = count.bit_length() - 1
     extra = 2 * depth - 1
     return pl.pallas_call(
-        local_kernel,
+        functools.partial(tree_kernel, spread),
+        in_specs=[pl.BlockSpec(memory_space=pltpu.VMEM)] * 2,
+        out_specs=[pl.BlockSpec(memory_space=pltpu.VMEM)] * 2,
         out_shape=[
             jax.ShapeDtypeStruct(compact.shape, jnp.bfloat16),
-            jax.ShapeDtypeStruct((depth, samples, samples), jnp.bfloat16),
+            jax.ShapeDtypeStruct((1, depth + spread, samples, samples), jnp.bfloat16),
         ],
         scratch_shapes=[
-            pltpu.VMEM((count + extra, half, samples), jnp.float32),
+            pltpu.VMEM((count + extra + 2 * spread, half, samples), jnp.float32),
             pltpu.VMEM((extra, half, samples), jnp.float32),
-            pltpu.VMEM((2 * depth, half, samples), jnp.float32),
+            pltpu.VMEM((2 + extra + 2 * spread - 1, half, samples), jnp.float32),
+            pltpu.VMEM((spread + 1, half, double), jnp.float32),
+            pltpu.VMEM((spread, half, double), jnp.float32),
+            pltpu.SemaphoreType.DMA((spread,)),
+            pltpu.SemaphoreType.DMA((spread,)),
         ],
-        cost_estimate=pl.CostEstimate(
-            flops=500_000_000, bytes_accessed=4_000_000, transcendentals=0
-        ),
-        name="local",
+        compiler_params=pltpu.CompilerParams(collective_id=0, has_side_effects=True),
+        name="tree",
     )(grams, compact)
-
-
-def upper_kernel(nodes, level_out, work, uppers):
-    total = nodes.shape[0]
-    half, samples = nodes.shape[1], nodes.shape[2] // 2
-    for node in range(total):
-        work[node] = start_matrix(nodes[node, :, :samples], half)
-    eliminate(total, half, work, uppers, {node: node for node in range(total - 1)})
-
-
-def upper_solve(nodes, picks, level_out, work, uppers):
-    upper_kernel(nodes, level_out, work, uppers)
-    total = nodes.shape[0]
-    samples = nodes.shape[2] // 2
-    spread = (total - 1) // 2
-    for height in range(spread):
-        if height == spread - 1:
-            answer = solved(work, total - 1, nodes[total - 1, :, samples:])
-        else:
-            mine = picks[height + 1]
-            place = 2 * (height + 1) + mine
-            answer = solved(work, place, nodes[place, :, samples:])
-        stacked = jnp.concatenate([uppers[2 * height], uppers[2 * height + 1]], axis=0)
-        level_out[height] = exact_dot(stacked, answer).astype(level_out.dtype)
-
-
-def upper_call(nodes, picks):
-    total, half, double = nodes.shape
-    samples = double // 2
-    spread = (total - 1) // 2
-    return pl.pallas_call(
-        upper_solve,
-        in_specs=[
-            pl.BlockSpec(memory_space=pltpu.VMEM),
-            pl.BlockSpec(memory_space=pltpu.SMEM),
-        ],
-        out_shape=jax.ShapeDtypeStruct((spread, samples, samples), jnp.bfloat16),
-        scratch_shapes=[
-            pltpu.VMEM((total, half, samples), jnp.float32),
-            pltpu.VMEM((total - 1, half, samples), jnp.float32),
-        ],
-        name="upper",
-    )(nodes, picks)
 
 
 def per_device(random_block, sample_block, near_blocks, near_index, near_count):
@@ -237,19 +250,7 @@
     grams, compact = gram_call(
         ids, near_count, near_blocks, sample_block, low, random_block, high
     )
-    summed = jnp.sum(grams, axis=0)
-    nodes = []
-    spread = size.bit_length() - 1
-    bits = (device >> jnp.arange(spread)) & 1
-    for step in range(spread):
-        other = lax.ppermute(summed, "boxes", [(i, i ^ (1 << step)) for i in range(size)])
-        odd = bits[step] == 1
-        nodes += [jnp.where(odd, other, summed), jnp.where(odd, summed, other)]
-        summed = summed + other
-    nodes.append(summed)
-    leaf_sketch, level_low = local_call(grams, compact)
-    level_high = upper_call(jnp.stack(nodes), bits.astype(jnp.int32))
-    return (leaf_sketch, jnp.concatenate([level_low, level_high], axis=0)[None])
+    return tuple(tree_call(grams, compact, size.bit_length() - 1))
 
 
 def solution(mesh):

time: 118 us -> 95.9 us (0.81)
  starting transfers between devices: 30.6 us -> 3.76 us
  Pallas kernels: 59.4 us -> 80.5 us
  waiting for transfers between devices: 16.1 us -> 4.12 us
  between operations: 3.98 us -> 0.67 us
  other arithmetic: 3.87 us -> 0.69 us
  local copies, waits for them, and re-layouts: 3.2 us -> 5.65 us
    ppermute x5 -> x0, starting transfers between devices: 26.9 us -> none  [per_device(): lax.ppermute(summed, 'boxes', [(i, i ^ 1 << step) for i in range(size)])]
    pallas_call x2 -> x1, Pallas kernels: 41.7 us -> 62.8 us  [tree_call(): pl.pallas_call(functools.partial(tree_kernel, spread), in_specs=[pl.Block...]
    ppermute x5 -> x0, waiting for transfers between devices: 12 us -> none  [per_device(): lax.ppermute(summed, 'boxes', [(i, i ^ 1 << step) for i in range(size)])]
    unnamed x8 -> x6, local copies, waits for them, and re-layouts: 1.87 us -> 4.97 us
    broadcast_in_dim x1 -> x0, other arithmetic: 1.72 us -> none  [per_device(): return (leaf_sketch, jnp.concatenate([level_low, level_high], axis=0)[None])]
    reduce_sum x1 -> x0, other arithmetic: 1.29 us -> none  [per_device(): summed = jnp.sum(grams, axis=0)]
  transfers between devices with their start and end apart: 7 -> 2, of which waited for: 5 -> 1; matrix products, arithmetic and copies ran while one was open for 2% -> 1% of each run, Pallas kernels for 22% -> 0%
where the time goes in v3:
time: 95.9 us; the launch traced here: 95.4 us
  Pallas kernels  80.5 us (84%)
  local copies, waits for them, and re-layouts  5.65 us (6%)
  waiting for transfers between devices  4.12 us (4%)
  starting transfers between devices  3.76 us (4%)
    pallas_call x1, Pallas kernels, tree_call(): pl.pallas_call(functools.partial(tree_kernel, spread), in_specs=[pl.Block...  62.8 us
    pallas_call x1, Pallas kernels, gram_call(): pl.pallas_call(gram_kernel, grid_spec=pltpu.PrefetchScalarGridSpec(num_sc...  17.7 us
    unnamed x6, local copies, waits for them, and re-layouts  4.97 us
    ppermute x1, waiting for transfers between devices, per_device(): high = lax.ppermute(random_block, 'boxes', backward)  4.11 us
    ppermute x1, starting transfers between devices, per_device(): low = lax.ppermute(random_block, 'boxes', forward)  2.47 us
  transfers between devices with their start and end apart: 2, of which 1 were waited for; matrix products, arithmetic and copies ran while one was open for 1% of the time, Pallas kernels for 0%

profile of v3, /device:TPU:0, one launch (start us, length us, event | category | flops | bytes accessed | tf_op | source)
XLA Modules:
  0.0 95.4 jit_solution(11535794230019994945)
XLA Ops:
  0.6 2.5 %collective-permute-start = (bf16[16,256,128]{2,1,0:T(8,128)(2,1)}, bf16[16,256,128]{2,1,0:T(8,128)(2,1)S(1)}, u32[]{:S(2)}, u32[]{:S(2)}) collective-permute-start(bf16[16,256,128]{2,1,0:T(8,128)(2,1)} %own.1), channel_id=1, source_target_pairs={{0,1},{1,2},{2,3},{3,4},{4,5},{5,6},{6,7},{7,8},{8,9},{9,10},{10,1... | collective-permute-start | bytes 3145736 | tf_op jit(solution)/shard_map/ppermute | solution.py:247
  3.1 1.3 %collective-permute-start.1 = (bf16[16,256,128]{2,1,0:T(8,128)(2,1)}, bf16[16,256,128]{2,1,0:T(8,128)(2,1)S(1)}, u32[]{:S(2)}, u32[]{:S(2)}) collective-permute-start(bf16[16,256,128]{2,1,0:T(8,128)(2,1)} %own.1), channel_id=1, source_target_pairs={{1,0},{2,1},{3,2},{4,3},{5,4},{6,5},{7,6},{8,7},{9,8},{10,9},{11,1... | collective-permute-start | bytes 3145736 | tf_op jit(solution)/shard_map/ppermute | solution.py:248
  4.4 0.7 add_clamp_fusion
  5.1 0.1 copy.8
  5.2 0.6 reshape.7.ids
  5.8 0.0 collective-permute-done.low
  5.8 0.0 copy-start
  5.8 4.1 %collective-permute-done.1.high = bf16[16,256,128]{2,1,0:T(8,128)(2,1)S(1)} collective-permute-done((bf16[16,256,128]{2,1,0:T(8,128)(2,1)}, bf16[16,256,128]{2,1,0:T(8,128)(2,1)S(1)}, u32[]{:S(2)}, u32[]{:S(2)}) %collective-permute-start.1) | collective-permute-done | bytes 1048608 | tf_op jit(solution)/shard_map/ppermute | solution.py:248
  9.9 0.0 copy-done
  9.9 0.0 copy-start.1
  9.9 1.0 %copy-done.1 = bf16[16,256,128]{2,1,0:T(8,128)(2,1)} copy-done((bf16[16,256,128]{2,1,0:T(8,128)(2,1)}, bf16[16,256,128]{2,1,0:T(8,128)(2,1)S(1)}, u32[]{:S(2)}) %copy-start.1) | copy-done | bytes 1048600
  10.9 17.7 %gram.1 = (f32[16,64,256]{2,1,0:T(8,128)}, f32[16,256,128]{2,1,0:T(8,128)}) custom-call(s32[128]{0:T(128)} %reshape.7.ids, s32[16]{0:T(128)} %counts.1, bf16[16,8,256,256]{3,2,1,0:T(8,128)(2,1)} %blocks.1, bf16[16,256,128]{2,1,0:T(8,128)(2,1)} %sample.1, bf16[16,256,128]{2,1,0:T(8,128)(2,1)} %copy-done, bf16[16,256,128]{2,1,0:T(8,128)(2,1)} %own.1, ...), custom_call_target="tpu_custom_call" | custom-call | tf_op jit(solution)/shard_map/gram/pallas_call | solution.py:55
  28.6 62.8 %tree.1 = (bf16[16,256,128]{2,1,0:T(8,128)(2,1)}, bf16[1,9,128,128]{3,2,1,0:T(8,128)(2,1)}) custom-call(f32[16,64,256]{2,1,0:T(8,128)} %get-tuple-element.4.grams, f32[16,256,128]{2,1,0:T(8,128)} %get-tuple-element.5.compact), custom_call_target="tpu_custom_call" | custom-call | tf_op jit(solution)/shard_map/tree/pallas_call | solution.py:219
  91.4 2.3 %copy.11 = bf16[16,256,128]{2,1,0:T(8,128)(2,1)} copy(bf16[16,256,128]{2,1,0:T(8,128)(2,1)} %get-tuple-element.8) | data formatting | bytes 2097152
  93.7 1.7 %copy.12 = bf16[1,9,128,128]{3,2,1,0:T(8,128)(2,1)} copy(bf16[1,9,128,128]{3,2,1,0:T(8,128)(2,1)} %get-tuple-element.9) | data formatting | bytes 589824
Async XLA Ops:
  0.6 5.2 %collective-permute-start = (bf16[16,256,128]{2,1,0:T(8,128)(2,1)}, bf16[16,256,128]{2,1,0:T(8,128)(2,1)S(1)}, u32[]{:S(2)}, u32[]{:S(2)}) collective-permute-start(bf16[16,256,128]{2,1,0:T(8,128)(2,1)} %own.1), channel_id=1, source_target_pairs={{0,1},{1,2},{2,3},{3,4},{4,5},{5,6},{6,7},{7,8},{8,9},{9,10},{10,1... | collective-permute-start | bytes 3145736 | tf_op jit(solution)/shard_map/ppermute | solution.py:247
  3.1 6.8 %collective-permute-start.1 = (bf16[16,256,128]{2,1,0:T(8,128)(2,1)}, bf16[16,256,128]{2,1,0:T(8,128)(2,1)S(1)}, u32[]{:S(2)}, u32[]{:S(2)}) collective-permute-start(bf16[16,256,128]{2,1,0:T(8,128)(2,1)} %own.1), channel_id=1, source_target_pairs={{1,0},{2,1},{3,2},{4,3},{5,4},{6,5},{7,6},{8,7},{9,8},{10,9},{11,1... | collective-permute-start | bytes 3145736 | tf_op jit(solution)/shard_map/ppermute | solution.py:248
  5.8 4.1 %copy-start = (bf16[16,256,128]{2,1,0:T(8,128)(2,1)}, bf16[16,256,128]{2,1,0:T(8,128)(2,1)S(1)}, u32[]{:S(2)}) copy-start(bf16[16,256,128]{2,1,0:T(8,128)(2,1)S(1)} %collective-permute-done.low) | copy-start | bytes 3145732
  9.9 1.0 %copy-start.1 = (bf16[16,256,128]{2,1,0:T(8,128)(2,1)}, bf16[16,256,128]{2,1,0:T(8,128)(2,1)S(1)}, u32[]{:S(2)}) copy-start(bf16[16,256,128]{2,1,0:T(8,128)(2,1)S(1)} %collective-permute-done.1.high) | copy-start | bytes 3145732

commit v4 on v3

--- a/solution.py
+++ b/solution.py
@@ -50,7 +50,7 @@
     count, rows, samples = sample.shape
     slots = blocks.shape[1]
     half = samples // 2
-    together = 2 if count % 2 == 0 else 1
+    together = 4 if count % 4 == 0 else 1
     anywhere = pl.BlockSpec(memory_space=pl.ANY)
     return pl.pallas_call(
         gram_kernel,

time: 95.9 us -> 95.4 us (level)
  no operation moved by 1% of the time
where the time goes in v4:
time: 95.4 us; the launch traced here: 95.1 us
  Pallas kernels  80.2 us (84%)
  local copies, waits for them, and re-layouts  5.65 us (6%)
  waiting for transfers between devices  4.12 us (4%)
  starting transfers between devices  3.76 us (4%)
    pallas_call x1, Pallas kernels, tree_call(): pl.pallas_call(functools.partial(tree_kernel, spread), in_specs=[pl.Block...  62.8 us
    pallas_call x1, Pallas kernels, gram_call(): pl.pallas_call(gram_kernel, grid_spec=pltpu.PrefetchScalarGridSpec(num_sc...  17.5 us
    unnamed x6, local copies, waits for them, and re-layouts  4.97 us
    ppermute x1, waiting for transfers between devices, per_device(): high = lax.ppermute(random_block, 'boxes', backward)  4.11 us
    ppermute x1, starting transfers between devices, per_device(): low = lax.ppermute(random_block, 'boxes', forward)  2.47 us
  transfers between devices with their start and end apart: 2, of which 1 were waited for; matrix products, arithmetic and copies ran while one was open for 1% of the time, Pallas kernels for 0%

profile of v4, /device:TPU:0, one launch (start us, length us, event | category | flops | bytes accessed | tf_op | source)
XLA Modules:
  0.0 95.1 jit_solution(18241788667830198531)
XLA Ops:
  0.6 2.5 %collective-permute-start = (bf16[16,256,128]{2,1,0:T(8,128)(2,1)}, bf16[16,256,128]{2,1,0:T(8,128)(2,1)S(1)}, u32[]{:S(2)}, u32[]{:S(2)}) collective-permute-start(bf16[16,256,128]{2,1,0:T(8,128)(2,1)} %own.1), channel_id=1, source_target_pairs={{0,1},{1,2},{2,3},{3,4},{4,5},{5,6},{6,7},{7,8},{8,9},{9,10},{10,1... | collective-permute-start | bytes 3145736 | tf_op jit(solution)/shard_map/ppermute | solution.py:247
  3.1 1.3 %collective-permute-start.1 = (bf16[16,256,128]{2,1,0:T(8,128)(2,1)}, bf16[16,256,128]{2,1,0:T(8,128)(2,1)S(1)}, u32[]{:S(2)}, u32[]{:S(2)}) collective-permute-start(bf16[16,256,128]{2,1,0:T(8,128)(2,1)} %own.1), channel_id=1, source_target_pairs={{1,0},{2,1},{3,2},{4,3},{5,4},{6,5},{7,6},{8,7},{9,8},{10,9},{11,1... | collective-permute-start | bytes 3145736 | tf_op jit(solution)/shard_map/ppermute | solution.py:248
  4.4 0.7 add_clamp_fusion
  5.1 0.1 copy.8
  5.2 0.6 reshape.7.ids
  5.8 0.0 collective-permute-done.low
  5.8 0.0 copy-start
  5.8 4.1 %collective-permute-done.1.high = bf16[16,256,128]{2,1,0:T(8,128)(2,1)S(1)} collective-permute-done((bf16[16,256,128]{2,1,0:T(8,128)(2,1)}, bf16[16,256,128]{2,1,0:T(8,128)(2,1)S(1)}, u32[]{:S(2)}, u32[]{:S(2)}) %collective-permute-start.1) | collective-permute-done | bytes 1048608 | tf_op jit(solution)/shard_map/ppermute | solution.py:248
  9.9 0.0 copy-done
  9.9 0.0 copy-start.1
  9.9 1.0 %copy-done.1 = bf16[16,256,128]{2,1,0:T(8,128)(2,1)} copy-done((bf16[16,256,128]{2,1,0:T(8,128)(2,1)}, bf16[16,256,128]{2,1,0:T(8,128)(2,1)S(1)}, u32[]{:S(2)}) %copy-start.1) | copy-done | bytes 1048600
  10.9 17.5 %gram.1 = (f32[16,64,256]{2,1,0:T(8,128)}, f32[16,256,128]{2,1,0:T(8,128)}) custom-call(s32[128]{0:T(128)} %reshape.7.ids, s32[16]{0:T(128)} %counts.1, bf16[16,8,256,256]{3,2,1,0:T(8,128)(2,1)} %blocks.1, bf16[16,256,128]{2,1,0:T(8,128)(2,1)} %sample.1, bf16[16,256,128]{2,1,0:T(8,128)(2,1)} %copy-done, bf16[16,256,128]{2,1,0:T(8,128)(2,1)} %own.1, ...), custom_call_target="tpu_custom_call" | custom-call | tf_op jit(solution)/shard_map/gram/pallas_call | solution.py:55
  28.3 62.8 %tree.1 = (bf16[16,256,128]{2,1,0:T(8,128)(2,1)}, bf16[1,9,128,128]{3,2,1,0:T(8,128)(2,1)}) custom-call(f32[16,64,256]{2,1,0:T(8,128)} %get-tuple-element.4.grams, f32[16,256,128]{2,1,0:T(8,128)} %get-tuple-element.5.compact), custom_call_target="tpu_custom_call" | custom-call | tf_op jit(solution)/shard_map/tree/pallas_call | solution.py:219
  91.1 2.3 %copy.11 = bf16[16,256,128]{2,1,0:T(8,128)(2,1)} copy(bf16[16,256,128]{2,1,0:T(8,128)(2,1)} %get-tuple-element.8) | data formatting | bytes 2097152
  93.4 1.7 %copy.12 = bf16[1,9,128,128]{3,2,1,0:T(8,128)(2,1)} copy(bf16[1,9,128,128]{3,2,1,0:T(8,128)(2,1)} %get-tuple-element.9) | data formatting | bytes 589824
Async XLA Ops:
  0.6 5.2 %collective-permute-start = (bf16[16,256,128]{2,1,0:T(8,128)(2,1)}, bf16[16,256,128]{2,1,0:T(8,128)(2,1)S(1)}, u32[]{:S(2)}, u32[]{:S(2)}) collective-permute-start(bf16[16,256,128]{2,1,0:T(8,128)(2,1)} %own.1), channel_id=1, source_target_pairs={{0,1},{1,2},{2,3},{3,4},{4,5},{5,6},{6,7},{7,8},{8,9},{9,10},{10,1... | collective-permute-start | bytes 3145736 | tf_op jit(solution)/shard_map/ppermute | solution.py:247
  3.1 6.8 %collective-permute-start.1 = (bf16[16,256,128]{2,1,0:T(8,128)(2,1)}, bf16[16,256,128]{2,1,0:T(8,128)(2,1)S(1)}, u32[]{:S(2)}, u32[]{:S(2)}) collective-permute-start(bf16[16,256,128]{2,1,0:T(8,128)(2,1)} %own.1), channel_id=1, source_target_pairs={{1,0},{2,1},{3,2},{4,3},{5,4},{6,5},{7,6},{8,7},{9,8},{10,9},{11,1... | collective-permute-start | bytes 3145736 | tf_op jit(solution)/shard_map/ppermute | solution.py:248
  5.8 4.1 %copy-start = (bf16[16,256,128]{2,1,0:T(8,128)(2,1)}, bf16[16,256,128]{2,1,0:T(8,128)(2,1)S(1)}, u32[]{:S(2)}) copy-start(bf16[16,256,128]{2,1,0:T(8,128)(2,1)S(1)} %collective-permute-done.low) | copy-start | bytes 3145732
  9.9 1.0 %copy-start.1 = (bf16[16,256,128]{2,1,0:T(8,128)(2,1)}, bf16[16,256,128]{2,1,0:T(8,128)(2,1)S(1)}, u32[]{:S(2)}) copy-start(bf16[16,256,128]{2,1,0:T(8,128)(2,1)S(1)} %collective-permute-done.1.high) | copy-start | bytes 3145732
